TPU v7x, 128 devices: a whole 4x4x4 slice. The times are simulated.
128 devices in a mesh: dp: 8 (over x, core), ctx: 4 (over y), tensor: 4 (over z).
Axes of the slice: x: 4, y: 4, z: 4, core: 2. Of those that a mesh axis runs over, the one named last changes fastest.
Arguments:
- hidden: bfloat16 [8, 16384, 2560], P('dp', 'ctx', 'tensor'), may hold values from -6 to 6
- depth: int32 [8, 16384], P('dp', 'ctx'), may hold values from 1 to 4, as said below
- qkv_weight: bfloat16 [2560, 3, 2560], P(None, None, 'tensor'), may hold values from -0.125 to 0.125
- out_weight: bfloat16 [2560, 2560], P('tensor'), may hold values from -0.125 to 0.125
Outputs:
- update: bfloat16 [8, 16384, 2560], P('dp', 'ctx', 'tensor')
Inputs may be any that keep to these rules, and one draw needn't show every extreme that they name: In every aligned block of 4096 positions of a document at most 1024 tokens have depth at least 3, and some block has exactly 1024; over all documents exactly 16384 tokens do.
All inputs are finite; a program needn't handle non-finite values.
Results may differ from a plain program's by a relative error of at most 0.012.
The roundings to bfloat16 on the way count: a program that leaves them out, or rounds other values in their place, can miss the bound.
Values may be sent and summed in bfloat16 or wider, within the bound.
No kernel may reach another device: no remote copies, remote signals or barrier semaphores. Data moves between devices by JAX's collectives and lax.ppermute only.
A program may use at most 256 MiB of HBM per device.

v0:
```python
import jax
import jax.numpy as jnp
from jax import lax
from jax.sharding import PartitionSpec as P

HD = 128
RECURSION = 3
ACT_DEV = 512
CAP = 1024
score_scale = 0.25
norm_epsilon = 1e-05
head_epsilon = 1e-06


def head_normed(values):
    row_count = values.shape[0]
    per_head = values.reshape(row_count, -1, HD)
    factor = lax.rsqrt(jnp.mean(per_head * per_head, axis=2, keepdims=True) + head_epsilon)
    return (per_head * factor).reshape(row_count, -1).astype(jnp.bfloat16)


def project_rows(token_rows, qkv_weight):
    full_rows = lax.all_gather(token_rows, "tensor", axis=1, tiled=True)
    widened = full_rows.astype(jnp.float32)
    factor = lax.rsqrt(jnp.mean(widened * widened, axis=1, keepdims=True) + norm_epsilon)
    normed = (widened * factor).astype(jnp.bfloat16)
    head_width = qkv_weight.shape[2]
    projection = jnp.dot(
        normed,
        qkv_weight.reshape(qkv_weight.shape[0], 3 * head_width),
        preferred_element_type=jnp.float32,
    )
    queries = head_normed(projection[:, :head_width])
    keys_normed = head_normed(projection[:, head_width : 2 * head_width])
    values_out = projection[:, 2 * head_width :].astype(jnp.bfloat16)
    return jnp.concatenate([queries, keys_normed, values_out], axis=1)


def output_rows(context, out_weight):
    partial_value = jnp.dot(context, out_weight, preferred_element_type=jnp.float32)
    return lax.psum_scatter(
        partial_value.astype(jnp.bfloat16), "tensor", scatter_dimension=1, tiled=True
    )


def move_tiles(payload):
    return lax.all_to_all(payload, ("dp", "ctx"), split_axis=0, concat_axis=0, tiled=True)


def per_device(hidden, depth, qkv_weight, out_weight):
    tokens = hidden[0]
    local_len = tokens.shape[0]
    feature_width = tokens.shape[1]
    capacity = CAP
    head_width = out_weight.shape[0]
    heads_here = head_width // HD
    ctx_count = lax.axis_size("ctx")
    spread_size = lax.axis_size("dp") * ctx_count
    ctx_rank = lax.axis_index("ctx")
    my_index = lax.axis_index("dp") * ctx_count + ctx_rank
    active = (depth[0] >= RECURSION).astype(jnp.int32)
    active_count = jnp.sum(active)
    active_rank = jnp.cumsum(active) - 1
    slot_token = (
        jnp.zeros((capacity,), jnp.int32)
        .at[jnp.where(active > 0, active_rank, capacity)]
        .set(jnp.arange(local_len, dtype=jnp.int32), mode="drop")
    )
    filled = jnp.arange(capacity, dtype=jnp.int32) < active_count
    token_rows = jnp.where(filled[:, None], tokens[slot_token], jnp.zeros((), tokens.dtype))
    counts = lax.all_gather(active_count[None], ("dp", "ctx"), axis=0, tiled=True)
    doc_counts = lax.dynamic_slice_in_dim(counts, lax.axis_index("dp") * ctx_count, ctx_count)
    slot_size = capacity // spread_size
    offsets = jnp.cumsum(counts) - counts
    first_rank = offsets[my_index]
    global_rank = first_rank + jnp.arange(capacity, dtype=jnp.int32)
    target = global_rank % spread_size
    position = (
        global_rank // spread_size
        - first_rank // spread_size
        - (target < first_rank % spread_size).astype(jnp.int32)
    )
    send_at = jnp.where(filled, target * slot_size + position, capacity)
    fetch_at = jnp.minimum(send_at, capacity - 1)
    lower_bound = (offsets - my_index + spread_size - 1) // spread_size
    upper_bound = (offsets + counts - my_index + spread_size - 1) // spread_size
    arrived = (
        jnp.arange(slot_size, dtype=jnp.int32)[None, :] < (upper_bound - lower_bound)[:, None]
    ).reshape(-1)
    arrived_rank = jnp.cumsum(arrived.astype(jnp.int32)) - 1
    chosen = (
        jnp.zeros((ACT_DEV,), jnp.int32)
        .at[jnp.where(arrived, arrived_rank, ACT_DEV)]
        .set(jnp.arange(capacity, dtype=jnp.int32), mode="drop")
    )
    packed = (
        jnp.zeros((capacity,) + token_rows.shape[1:], token_rows.dtype)
        .at[send_at]
        .set(token_rows, mode="drop")
    )
    values = project_rows(move_tiles(packed)[chosen], qkv_weight)
    bring_packed = jnp.zeros((capacity,) + values.shape[1:], values.dtype).at[chosen].set(values)
    projected = move_tiles(bring_packed)[fetch_at]
    queries = projected[:, :head_width]
    key_values = projected[:, head_width:]
    query_heads = queries.reshape(capacity, heads_here, HD)
    key_piece = lax.all_gather(key_values, "ctx", axis=0, tiled=True)
    piece_rows = key_piece.shape[0]
    row_index = jnp.arange(piece_rows, dtype=jnp.int32)
    source_shard = row_index // capacity
    source_slot = row_index - source_shard * capacity
    clipped = jnp.clip(source_shard, 0, ctx_count - 1)
    key_filled = (source_shard >= 0) & (source_slot < doc_counts[clipped])
    same_block = (source_shard == ctx_rank)[None, :] & (
        slot_token[source_slot][None, :] <= slot_token[:, None]
    )
    earlier = (source_shard < ctx_rank)[None, :] | same_block
    allowed = earlier & key_filled[None, :] & filled[:, None]
    key_heads = key_piece[:, :head_width].reshape(piece_rows, heads_here, HD)
    value_heads = key_piece[:, head_width:].reshape(piece_rows, heads_here, HD)
    scores = (
        jnp.einsum("qhd,khd->hqk", query_heads, key_heads, preferred_element_type=jnp.float32)
        * score_scale
    )
    weights = jnp.where(allowed[None], jnp.exp(scores), 0.0)
    numerator = jnp.einsum(
        "hqk,khd->qhd",
        weights.astype(jnp.bfloat16),
        value_heads,
        preferred_element_type=jnp.float32,
    )
    denominator = jnp.sum(weights, axis=2)
    numerator, denominator = (numerator, denominator)
    guarded = denominator + (1.0 - filled.astype(jnp.float32))[None, :]
    context = (
        (numerator / jnp.transpose(guarded)[:, :, None])
        .reshape(capacity, head_width)
        .astype(jnp.bfloat16)
    )
    result_rows = output_rows(context, out_weight)
    update = (
        jnp.zeros((local_len, feature_width), jnp.bfloat16)
        .at[jnp.where(filled, slot_token, local_len)]
        .set(result_rows, mode="drop")
    )
    return update[None]


def solution(mesh):
    placed = (P("dp", "ctx", "tensor"), P("dp", "ctx"), P(None, None, "tensor"), P("tensor", None))
    return jax.shard_map(
        per_device, mesh=mesh, in_specs=placed, out_specs=P("dp", "ctx", "tensor"), check_vma=False
    )
```

profile of v0, /device:TPU:1, one launch (start us, length us, event | category | flops | bytes accessed | tf_op | source)
XLA Modules:
  0.0 554.3 jit_solution(16296913542401398679)
XLA Ops:
  11.6 16.9 %all-reduce = s32[32]{0:T(128)S(1)} all-reduce(s32[32]{0:T(128)S(1)} %dynamic-update-slice), channel_id=1, replica_groups=mesh['dp'=8,'ctx'=4,'tensor'=4] {'dp','ctx'}, use_global_device_ids=true, to_apply=%add | all-reduce | flops 32 | bytes 256
  33.9 15.5 %scatter_custom_fusion = s32[1024]{0:T(1024)S(1)} fusion(s32[4096]{0:T(1024)S(1)} %bitcast.67, s32[4096]{0:T(1024)S(1)} %iota.52, s32[]{:T(128)} %constant.133.clone.1), kind=kCustom, calls=%fused_computation.99 | custom fusion | bytes 4100 | tf_op jit(solution)/shard_map/scatter | solution.py:67
  52.0 37.8 %scatter_custom_fusion.2 = bf16[1024,640]{1,0:T(8,128)(2,1)} fusion(s32[1024]{0:T(1024)S(1)} %bitcast.71, pred[1024]{0:T(1024)(128)(4,1)S(1)} %iota_compare_fusion.1, bf16[]{:T(256)} %constant.131.clone.1, bf16[4096,640]{1,0:T(8,128)(2,1)} %bitcast.59, s32[1024]{0:T(1024)S(1)} %get-tuple-element.13), kind=kCustom, calls=%fused_computation.37 | custom fusion | flops 655360 | bytes 6559744 | tf_op jit(solution)/shard_map/scatter | solution.py:99
  89.8 12.2 %all-to-all-start = ((bf16[32,32,640]{2,1,0:T(8,128)(2,1)}), bf16[32,32,640]{2,1,0:T(8,128)(2,1)}, u32[]{:S(2)}, u32[]{:S(2)}) async-start(bf16[32,32,640]{2,1,0:T(8,128)(2,1)} %bitcast.60), calls=%async_computation | async-start | bytes 2621440 | tf_op jit(solution)/shard_map/all_to_all | solution.py:47
  107.9 13.0 %all-to-all-done = bf16[32,32,640]{2,1,0:T(8,128)(2,1)} async-done(((bf16[32,32,640]{2,1,0:T(8,128)(2,1)}), bf16[32,32,640]{2,1,0:T(8,128)(2,1)}, u32[]{:S(2)}, u32[]{:S(2)}) %all-to-all-start) | async-done | bytes 1310752 | tf_op jit(solution)/shard_map/all_to_all | solution.py:47
  125.2 13.9 %copy.19 = bf16[2560,3,640]{0,2,1:T(8,128)(2,1)} copy(bf16[2560,3,640]{2,0,1:T(8,128)(2,1)} %param.6) | data formatting | bytes 19660800 | tf_op args[2]
  139.1 21.1 %all-gather.6.cloned.1.call-done = bf16[512,2560]{1,0:T(8,128)(2,1)} async-done(((bf16[512,640]{1,0:T(8,128)(2,1)}), bf16[512,2560]{1,0:T(8,128)(2,1)}) %all-gather.6.cloned.1.call-update) | async-done | bytes 2621456 | tf_op jit(solution)/shard_map/all_gather | solution.py:23
  162.5 9.3 %fusion.7 = f32[512,1920]{1,0:T(8,128)S(1)} fusion(bf16[2560,1920]{0,1:T(8,128)(2,1)} %bitcast.52, bf16[512,2560]{1,0:T(8,128)(2,1)} %all-gather.6.cloned.1.call-done, f32[512]{0:T(512)S(1)} %add_rsqrt_fusion.2), kind=kOutput, calls=%fused_computation.20 | convolution fusion | flops 5037096960 | bytes 16386048 | tf_op jit(solution)/shard_map/dot_general | solution.py:28
  196.1 7.0 %scatter_custom_fusion.3 = bf16[1024,1920]{1,0:T(8,128)(2,1)} fusion(s32[512]{0:T(512)S(1)} %compare_select_fusion.15, bf16[512,640]{1,0:T(8,128)(2,1)} %slice.81, bf16[]{:T(256)} %constant.171, bf16[512,640]{1,0:T(8,128)(2,1)} %get-tuple-element.10, bf16[512,640]{1,0:T(8,128)(2,1)} %get-tuple-element.9, bf16[]{:T(256)} %constant.131.clone.1), kind=kCustom, calls=%fused_computation.26 | custom fusion | flops 5898240 | bytes 5898244 | tf_op jit(solution)/shard_map/scatter | solution.py:102
  203.1 7.7 %all-to-all-start.1 = ((bf16[32,32,1920]{2,1,0:T(8,128)(2,1)}), bf16[32,32,1920]{2,1,0:T(8,128)(2,1)}, u32[]{:S(2)}, u32[]{:S(2)}) async-start(bf16[32,32,1920]{2,1,0:T(8,128)(2,1)} %bitcast.51), calls=%async_computation.1 | async-start | bytes 7864320 | tf_op jit(solution)/shard_map/all_to_all | solution.py:47
  210.9 47.3 %all-to-all-done.1 = bf16[32,32,1920]{2,1,0:T(8,128)(2,1)} async-done(((bf16[32,32,1920]{2,1,0:T(8,128)(2,1)}), bf16[32,32,1920]{2,1,0:T(8,128)(2,1)}, u32[]{:S(2)}, u32[]{:S(2)}) %all-to-all-start.1) | async-done | bytes 3932192 | tf_op jit(solution)/shard_map/all_to_all | solution.py:47
  258.2 11.1 %gather_fusion.1 = bf16[1024,1920]{1,0:T(8,128)(2,1)} fusion(bf16[1024,1920]{1,0:T(8,128)(2,1)} %bitcast.20, s32[1024]{0:T(1024)S(1)} %broadcast_clamp_fusion.1), kind=kCustom, calls=%fused_computation.2 | custom fusion | bytes 7868416 | tf_op jit(solution)/shard_map/gather | solution.py:103
  272.8 16.7 %gather_fusion.2 = s32[4096]{0:T(1024)S(1)} fusion(s32[1024]{0:T(1024)S(1)} %scatter_custom_fusion, s32[4096]{0:T(1024)S(1)} %broadcast_clamp_fusion), kind=kCustom, calls=%fused_computation.3 | custom fusion | bytes 49152 | tf_op jit(solution)/shard_map/gather | solution.py:115
  293.3 6.2 %and_and_fusion = pred[1024,4096]{1,0:T(8,128)(4,1)} fusion(s32[4096]{0:T(1024)S(1)} %gather_fusion.2, s32[1024]{0:T(1024)S(1)} %scatter_custom_fusion, pred[1024]{0:T(1024)(128)(4,1)S(1)} %iota_compare_fusion.1, pred[4096]{0:T(1024)(128)(4,1)S(1)} %fusion.32, pred[4096]{0:T(1024)(128)(4,1)S(1)} %get-tuple-element.23, pred[4096]{0:T(1024)(128)(4,1)S(1)} %get-tuple-element.24), kind=kLoop, calls=%fused_computation.14 | loop fusion | flops 20971520 | bytes 4228096 | tf_op jit(solution)/shard_map/and | solution.py:118
  304.5 69.3 %all-gather.4.cloned.1.call-done = bf16[4096,1280]{1,0:T(8,128)(2,1)} async-done(((bf16[1024,1280]{1,0:T(8,128)(2,1)}), bf16[4096,1280]{1,0:T(8,128)(2,1)}) %all-gather.4.cloned.1.call-update) | async-done | bytes 10485776 | tf_op jit(solution)/shard_map/all_gather | solution.py:107
  373.8 9.0 %fusion.46 = (bf16[4096,640]{1,0:T(8,128)(2,1)}, bf16[4096,640]{1,0:T(8,128)(2,1)}) fusion(bf16[4096,1280]{1,0:T(8,128)(2,1)} %all-gather.4.cloned.1.call-done), kind=kLoop, calls=%fused_computation.116 | loop fusion | bytes 20971520 | tf_op jit(solution)/shard_map/slice | solution.py:119
  382.8 7.9 %copy.24 = bf16[4096,640]{0,1:T(8,128)(2,1)} copy(bf16[4096,640]{1,0:T(8,128)(2,1)} %get-tuple-element.8) | data formatting | bytes 10485760 | tf_op jit(solution)/shard_map/slice | solution.py:120
  390.8 8.0 %copy.26 = bf16[4096,640]{0,1:T(8,128)(2,1)} copy(bf16[4096,640]{1,0:T(8,128)(2,1)} %get-tuple-element.7) | data formatting | bytes 10485760 | tf_op jit(solution)/shard_map/slice | solution.py:119
  398.8 36.3 %fusion = (f32[5,1024]{1,0:T(8,128)S(1)}, f32[5,1024,4096]{2,1,0:T(8,128)}) fusion(pred[1024,4096]{1,0:T(8,128)(4,1)} %and_and_fusion, bf16[1024,5,128]{0,2,1:T(8,128)(2,1)} %bitcast.61, bf16[4096,5,128]{0,2,1:T(8,128)(2,1)} %bitcast.54), kind=kOutput, calls=%fused_computation.10 | convolution fusion | flops 5431618560 | bytes 94654464 | tf_op jit(solution)/shard_map/qhd,khd->hqk/dot_general | solution.py:122
  435.1 30.0 %fusion.9 = bf16[1024,5,128]{0,2,1:T(8,128)(2,1)S(1)} fusion(bf16[4096,5,128]{0,2,1:T(8,128)(2,1)} %bitcast.53, f32[5,1024,4096]{2,1,0:T(8,128)} %get-tuple-element.20, pred[1024,4096]{1,0:T(8,128)(4,1)} %and_and_fusion, f32[1024,5]{0,1:T(8,128)S(1)} %add_bitcast_fusion), kind=kOutput, calls=%fused_computation.22 | convolution fusion | flops 5432934400 | bytes 94654464 | tf_op jit(solution)/shard_map/hqk,khd->qhd/dot_general | solution.py:126
  465.1 6.3 %convolution_convert_fusion = bf16[1024,2560]{1,0:T(8,128)(2,1)} fusion(bf16[1024,640]{0,1:T(8,128)(2,1)S(1)} %bitcast.73, bf16[640,2560]{1,0:T(8,128)(2,1)S(1)} %copy-done), kind=kOutput, calls=%fused_computation.17 | convolution fusion | flops 3358064640 | bytes 9830400 | tf_op jit(solution)/shard_map/dot_general | solution.py:40
  471.4 8.0 %copy.31 = bf16[1024,2560]{0,1:T(8,128)(2,1)} copy(bf16[1024,2560]{1,0:T(8,128)(2,1)} %convolution_convert_fusion) | data formatting | bytes 10485760
  479.4 56.8 %reduce-scatter.4.cloned.1.call-done = bf16[640,1024]{1,0:T(8,128)(2,1)} async-done(((bf16[2560,1024]{1,0:T(8,128)(2,1)}), bf16[640,1024]{1,0:T(8,128)(2,1)}) %reduce-scatter.4.cloned.1.call-update) | async-done | bytes 1310736
  538.6 9.0 %scatter_custom_fusion.4 = bf16[4096,640]{1,0:T(8,128)(2,1)} fusion(s32[1024]{0:T(1024)} %get-tuple-element.14, bf16[1024,640]{1,0:T(8,128)(2,1)} %copy.32, bf16[]{:T(256)} %constant.131.clone.1), kind=kCustom, calls=%fused_computation.24 | custom fusion | bytes 5243392 | tf_op jit(solution)/shard_map/scatter | solution.py:144
  (78 shorter events, 61.9 us)
Async XLA Ops:
  6.5 458.6 %copy-start = (bf16[640,2560]{1,0:T(8,128)(2,1)S(1)}, bf16[640,2560]{1,0:T(8,128)(2,1)}, u32[]{:S(2)}) copy-start(bf16[640,2560]{1,0:T(8,128)(2,1)} %param.7) | copy-start | bytes 9830404
  89.8 31.1 %all-to-all-start = ((bf16[32,32,640]{2,1,0:T(8,128)(2,1)}), bf16[32,32,640]{2,1,0:T(8,128)(2,1)}, u32[]{:S(2)}, u32[]{:S(2)}) async-start(bf16[32,32,640]{2,1,0:T(8,128)(2,1)} %bitcast.60), calls=%async_computation | async-start | bytes 2621440 | tf_op jit(solution)/shard_map/all_to_all | solution.py:47
  102.0 58.2 %all-gather.6.cloned.1.call-start = ((), (), s32[]{:S(2)}) async-start(), calls=%async_computation.4 | async-start | bytes 3276800 | tf_op jit(solution)/shard_map/all_gather | solution.py:23
  171.8 2.1 copy-start.1
  203.1 55.1 %all-to-all-start.1 = ((bf16[32,32,1920]{2,1,0:T(8,128)(2,1)}), bf16[32,32,1920]{2,1,0:T(8,128)(2,1)}, u32[]{:S(2)}, u32[]{:S(2)}) async-start(bf16[32,32,1920]{2,1,0:T(8,128)(2,1)} %bitcast.51), calls=%async_computation.1 | async-start | bytes 7864320 | tf_op jit(solution)/shard_map/all_to_all | solution.py:47
  210.8 163.0 %all-gather.4.cloned.1.call-start = ((), (), s32[]{:S(2)}) async-start(), calls=%async_computation.3 | async-start | bytes 13107200 | tf_op jit(solution)/shard_map/all_gather | solution.py:107
  272.7 263.4 %reduce-scatter.4.cloned.1.call-start = ((), (), s32[]{:S(2)}) async-start(), calls=%async_computation.5 | async-start | bytes 6553600
Sparse Core Ops, SparseCore 0:
  125.4 34.7 all-gather.5
  272.9 100.8 all-gather.3
  479.5 56.6 reduce-scatter.3
where the time goes:
time: 563 us; the launch traced here: 554 us
  waiting for transfers between devices  208 us (37%)
  local copies, waits for them, and re-layouts  140 us (25%)
  matrix products  81.8 us (15%)
  other arithmetic  72.3 us (13%)
  starting transfers between devices  20 us (4%)
  blocking collectives  16.9 us (3%)
  between operations  16.2 us (3%)
    all_gather x1, waiting for transfers between devices, per_device(): key_piece = lax.all_gather(key_values, 'ctx', axis=0, tiled=True)  69.3 us
    all_to_all x2, waiting for transfers between devices, move_tiles(): lax.all_to_all(payload, ('dp', 'ctx'), split_axis=0, concat_axis=0, tiled...  60.3 us
    unnamed x4, waiting for transfers between devices  56.9 us
    scatter x1, other arithmetic, per_device(): packed = jnp.zeros((capacity,) + token_rows.shape[1:], token_rows.dtype)....  37.8 us
    dot_general x1, matrix products, per_device(): jnp.einsum('qhd,khd->hqk', query_heads, key_heads, preferred_element_type...  36.3 us
    dot_general x1, matrix products, per_device(): jnp.einsum('hqk,khd->qhd', weights.astype(jnp.bfloat16), value_heads, pre...  30 us
    unnamed x10, local copies, waits for them, and re-layouts  28 us
    all_gather x1, waiting for transfers between devices, project_rows(): full_rows = lax.all_gather(token_rows, 'tensor', axis=1, tiled=True)  21.1 us
  transfers between devices with their start and end apart: 5, of which 5 were waited for; matrix products, arithmetic and copies ran while one was open for 9% of the time, Pallas kernels for 0%

commit v1 on v0

--- a/solution.py
+++ b/solution.py
@@ -104,7 +104,12 @@
     queries = projected[:, :head_width]
     key_values = projected[:, head_width:]
     query_heads = queries.reshape(capacity, heads_here, HD)
-    key_piece = lax.all_gather(key_values, "ctx", axis=0, tiled=True)
+    ring = [key_values]
+    for hop in range(3):
+        ring.append(lax.ppermute(ring[-1], "ctx", [(dev, (dev + 1) % 4) for dev in range(4)]))
+    key_piece = jnp.roll(
+        jnp.concatenate(ring[::-1], axis=0), (lax.axis_index("ctx") + 1) * ring[0].shape[0], axis=0
+    )
     piece_rows = key_piece.shape[0]
     row_index = jnp.arange(piece_rows, dtype=jnp.int32)
     source_shard = row_index // capacity

time: 563 us -> 659 us (1.17)
  waiting for transfers between devices: 208 us -> 279 us
  local copies, waits for them, and re-layouts: 140 us -> 161 us
    ppermute x0 -> x3, waiting for transfers between devices: none -> 143 us  [per_device(): lax.ppermute(ring[-1], 'ctx', [(dev, (dev + 1) % 4) for dev in range(4)])]
    all_gather x1 -> x0, waiting for transfers between devices: 69.3 us -> none  [per_device(): key_piece = lax.all_gather(key_values, 'ctx', axis=0, tiled=True)]
    unnamed x10 -> x23, local copies, waits for them, and re-layouts: 28 us -> 49.8 us
    unnamed x4 -> x3, waiting for transfers between devices: 56.9 us -> 54.9 us
  transfers between devices with their start and end apart: 5 -> 7, of which waited for: 5 -> 7; matrix products, arithmetic and copies ran while one was open for 9% -> 8% of each run, Pallas kernels for 0% -> 0%
where the time goes in v1:
time: 659 us; the launch traced here: 650 us
  waiting for transfers between devices  279 us (42%)
  local copies, waits for them, and re-layouts  161 us (24%)
  matrix products  81.9 us (12%)
  other arithmetic  72.4 us (11%)
  starting transfers between devices  21.3 us (3%)
  blocking collectives  16.9 us (3%)
  between operations  16.7 us (3%)
    ppermute x3, waiting for transfers between devices, per_device(): lax.ppermute(ring[-1], 'ctx', [(dev, (dev + 1) % 4) for dev in range(4)])  143 us
    all_to_all x2, waiting for transfers between devices, move_tiles(): lax.all_to_all(payload, ('dp', 'ctx'), split_axis=0, concat_axis=0, tiled...  60.6 us
    unnamed x3, waiting for transfers between devices  54.9 us
    unnamed x23, local copies, waits for them, and re-layouts  49.8 us
    scatter x1, other arithmetic, per_device(): packed = jnp.zeros((capacity,) + token_rows.shape[1:], token_rows.dtype)....  37.8 us
    dot_general x1, matrix products, per_device(): jnp.einsum('qhd,khd->hqk', query_heads, key_heads, preferred_element_type...  36.3 us
    dot_general x1, matrix products, per_device(): jnp.einsum('hqk,khd->qhd', weights.astype(jnp.bfloat16), value_heads, pre...  30.2 us
    all_gather x1, waiting for transfers between devices, project_rows(): full_rows = lax.all_gather(token_rows, 'tensor', axis=1, tiled=True)  21.1 us
  transfers between devices with their start and end apart: 7, of which 7 were waited for; matrix products, arithmetic and copies ran while one was open for 8% of the time, Pallas kernels for 0%

profile of v1, /device:TPU:1, one launch (start us, length us, event | category | flops | bytes accessed | tf_op | source)
XLA Modules:
  0.0 649.6 jit_solution(13747589565638169358)
XLA Ops:
  11.5 16.9 %all-reduce = s32[32]{0:T(128)S(1)} all-reduce(s32[32]{0:T(128)S(1)} %dynamic-update-slice), channel_id=1, replica_groups=mesh['dp'=8,'ctx'=4,'tensor'=4] {'dp','ctx'}, use_global_device_ids=true, to_apply=%add | all-reduce | flops 32 | bytes 256
  33.9 15.5 %scatter_custom_fusion = s32[1024]{0:T(1024)S(1)} fusion(s32[4096]{0:T(1024)S(1)} %bitcast.67, s32[4096]{0:T(1024)S(1)} %iota.52, s32[]{:T(128)} %constant.152.clone.1), kind=kCustom, calls=%fused_computation.107 | custom fusion | bytes 4100 | tf_op jit(solution)/shard_map/scatter | solution.py:67
  52.0 37.8 %scatter_custom_fusion.2 = bf16[1024,640]{1,0:T(8,128)(2,1)} fusion(s32[1024]{0:T(1024)S(1)} %bitcast.71, pred[1024]{0:T(1024)(128)(4,1)S(1)} %iota_compare_fusion.1, bf16[]{:T(256)} %constant.150.clone.1, bf16[4096,640]{1,0:T(8,128)(2,1)} %bitcast.59, s32[1024]{0:T(1024)S(1)} %get-tuple-element.13), kind=kCustom, calls=%fused_computation.37 | custom fusion | flops 655360 | bytes 6559744 | tf_op jit(solution)/shard_map/scatter | solution.py:99
  89.8 12.2 %all-to-all-start = ((bf16[32,32,640]{2,1,0:T(8,128)(2,1)}), bf16[32,32,640]{2,1,0:T(8,128)(2,1)}, u32[]{:S(2)}, u32[]{:S(2)}) async-start(bf16[32,32,640]{2,1,0:T(8,128)(2,1)} %bitcast.60), calls=%async_computation | async-start | bytes 2621440 | tf_op jit(solution)/shard_map/all_to_all | solution.py:47
  107.6 13.3 %all-to-all-done = bf16[32,32,640]{2,1,0:T(8,128)(2,1)} async-done(((bf16[32,32,640]{2,1,0:T(8,128)(2,1)}), bf16[32,32,640]{2,1,0:T(8,128)(2,1)}, u32[]{:S(2)}, u32[]{:S(2)}) %all-to-all-start) | async-done | bytes 1310752 | tf_op jit(solution)/shard_map/all_to_all | solution.py:47
  125.3 13.9 %copy.19 = bf16[2560,3,640]{0,2,1:T(8,128)(2,1)} copy(bf16[2560,3,640]{2,0,1:T(8,128)(2,1)} %param.6) | data formatting | bytes 19660800 | tf_op args[2]
  139.1 21.1 %all-gather.3.cloned.1.call-done = bf16[512,2560]{1,0:T(8,128)(2,1)} async-done(((bf16[512,640]{1,0:T(8,128)(2,1)}), bf16[512,2560]{1,0:T(8,128)(2,1)}) %all-gather.3.cloned.1.call-update) | async-done | bytes 2621456 | tf_op jit(solution)/shard_map/all_gather | solution.py:23
  162.5 9.3 %fusion.7 = f32[512,1920]{1,0:T(8,128)S(1)} fusion(bf16[2560,1920]{0,1:T(8,128)(2,1)} %bitcast.52, bf16[512,2560]{1,0:T(8,128)(2,1)} %all-gather.3.cloned.1.call-done, f32[512]{0:T(512)S(1)} %add_rsqrt_fusion.2), kind=kOutput, calls=%fused_computation.20 | convolution fusion | flops 5037096960 | bytes 16386048 | tf_op jit(solution)/shard_map/dot_general | solution.py:28
  196.1 7.0 %scatter_custom_fusion.3 = bf16[1024,1920]{1,0:T(8,128)(2,1)} fusion(s32[512]{0:T(512)S(1)} %compare_select_fusion.15, bf16[512,640]{1,0:T(8,128)(2,1)} %slice.81, bf16[]{:T(256)} %constant.200, bf16[512,640]{1,0:T(8,128)(2,1)} %get-tuple-element.10, bf16[512,640]{1,0:T(8,128)(2,1)} %get-tuple-element.9, bf16[]{:T(256)} %constant.150.clone.1), kind=kCustom, calls=%fused_computation.26 | custom fusion | flops 5898240 | bytes 5898244 | tf_op jit(solution)/shard_map/scatter | solution.py:102
  203.1 7.8 %all-to-all-start.1 = ((bf16[32,32,1920]{2,1,0:T(8,128)(2,1)}), bf16[32,32,1920]{2,1,0:T(8,128)(2,1)}, u32[]{:S(2)}, u32[]{:S(2)}) async-start(bf16[32,32,1920]{2,1,0:T(8,128)(2,1)} %bitcast.51), calls=%async_computation.1 | async-start | bytes 7864320 | tf_op jit(solution)/shard_map/all_to_all | solution.py:47
  210.9 47.3 %all-to-all-done.1 = bf16[32,32,1920]{2,1,0:T(8,128)(2,1)} async-done(((bf16[32,32,1920]{2,1,0:T(8,128)(2,1)}), bf16[32,32,1920]{2,1,0:T(8,128)(2,1)}, u32[]{:S(2)}, u32[]{:S(2)}) %all-to-all-start.1) | async-done | bytes 3932192 | tf_op jit(solution)/shard_map/all_to_all | solution.py:47
  258.2 11.1 %gather_fusion.1 = bf16[1024,1920]{1,0:T(8,128)(2,1)} fusion(bf16[1024,1920]{1,0:T(8,128)(2,1)} %bitcast.20, s32[1024]{0:T(1024)S(1)} %broadcast_clamp_fusion.1), kind=kCustom, calls=%fused_computation.2 | custom fusion | bytes 7868416 | tf_op jit(solution)/shard_map/gather | solution.py:103
  272.5 58.8 %collective-permute-done = bf16[1024,1280]{1,0:T(8,128)(2,1)S(1)} collective-permute-done((bf16[1024,1280]{1,0:T(8,128)(2,1)S(1)}, bf16[1024,1280]{1,0:T(8,128)(2,1)S(1)}, u32[]{:S(2)}, u32[]{:S(2)}) %collective-permute-start) | collective-permute-done | bytes 2621472 | tf_op jit(solution)/shard_map/ppermute | solution.py:109
  332.8 58.2 %collective-permute-done.1 = bf16[1024,1280]{1,0:T(8,128)(2,1)} collective-permute-done((bf16[1024,1280]{1,0:T(8,128)(2,1)S(1)}, bf16[1024,1280]{1,0:T(8,128)(2,1)}, u32[]{:S(2)}, u32[]{:S(2)}) %collective-permute-start.1) | collective-permute-done | bytes 2621472 | tf_op jit(solution)/shard_map/ppermute | solution.py:109
  391.1 16.7 %gather_fusion.2 = s32[4096]{0:T(1024)S(1)} fusion(s32[1024]{0:T(1024)S(1)} %scatter_custom_fusion, s32[4096]{0:T(1024)S(1)} %broadcast_clamp_fusion), kind=kCustom, calls=%fused_computation.3 | custom fusion | bytes 49152 | tf_op jit(solution)/shard_map/gather | solution.py:120
  422.9 25.7 %collective-permute-done.2 = bf16[1024,1280]{1,0:T(8,128)(2,1)} collective-permute-done((bf16[1024,1280]{1,0:T(8,128)(2,1)}, bf16[1024,1280]{1,0:T(8,128)(2,1)}, u32[]{:S(2)}, u32[]{:S(2)}) %collective-permute-start.2) | collective-permute-done | bytes 2621472 | tf_op jit(solution)/shard_map/ppermute | solution.py:109
  470.4 9.0 %constant_dynamic-slice_fusion = (bf16[4096,640]{1,0:T(8,128)(2,1)}, bf16[4096,640]{1,0:T(8,128)(2,1)}) fusion(bf16[8192,1280]{1,0:T(8,128)(2,1)} %constant_dynamic-update-slice_fusion, s32[]{:T(128)S(6)} %select_n.243, s32[]{:T(128)S(6)} %add.286), kind=kLoop, calls=%fused_computation.120 | loop fusion | bytes 20971528 | tf_op jit(solution)/shard_map/slice | solution.py:124
  479.4 7.9 %copy.24 = bf16[4096,640]{0,1:T(8,128)(2,1)} copy(bf16[4096,640]{1,0:T(8,128)(2,1)} %get-tuple-element.8) | data formatting | bytes 10485760 | tf_op jit(solution)/shard_map/slice | solution.py:125
  487.4 8.0 %copy.26 = bf16[4096,640]{0,1:T(8,128)(2,1)} copy(bf16[4096,640]{1,0:T(8,128)(2,1)} %get-tuple-element.7) | data formatting | bytes 10485760 | tf_op jit(solution)/shard_map/slice | solution.py:124
  495.4 36.3 %fusion = (f32[5,1024]{1,0:T(8,128)S(1)}, f32[5,1024,4096]{2,1,0:T(8,128)}) fusion(pred[1024,4096]{1,0:T(8,128)(4,1)} %and_and_fusion, bf16[1024,5,128]{0,2,1:T(8,128)(2,1)} %bitcast.61, bf16[4096,5,128]{0,2,1:T(8,128)(2,1)} %bitcast.54), kind=kOutput, calls=%fused_computation.10 | convolution fusion | flops 5431618560 | bytes 94654464 | tf_op jit(solution)/shard_map/qhd,khd->hqk/dot_general | solution.py:127
  531.7 30.2 %fusion.9 = bf16[1024,5,128]{0,2,1:T(8,128)(2,1)S(1)} fusion(bf16[4096,5,128]{0,2,1:T(8,128)(2,1)} %bitcast.53, f32[5,1024,4096]{2,1,0:T(8,128)} %get-tuple-element.20, pred[1024,4096]{1,0:T(8,128)(4,1)} %and_and_fusion, f32[1024,5]{0,1:T(8,128)S(1)} %add_bitcast_fusion), kind=kOutput, calls=%fused_computation.22 | convolution fusion | flops 5432934400 | bytes 94654464 | tf_op jit(solution)/shard_map/hqk,khd->qhd/dot_general | solution.py:131
  568.0 8.0 %copy.31 = bf16[1024,2560]{0,1:T(8,128)(2,1)} copy(bf16[1024,2560]{1,0:T(8,128)(2,1)} %convolution_convert_fusion) | data formatting | bytes 10485760
  576.0 54.9 %reduce-scatter.4.cloned.1.call-done = bf16[640,1024]{1,0:T(8,128)(2,1)} async-done(((bf16[2560,1024]{1,0:T(8,128)(2,1)}), bf16[640,1024]{1,0:T(8,128)(2,1)}) %reduce-scatter.4.cloned.1.call-update) | async-done | bytes 1310736
  633.3 9.0 %scatter_custom_fusion.4 = bf16[4096,640]{1,0:T(8,128)(2,1)} fusion(s32[1024]{0:T(1024)} %get-tuple-element.14, bf16[1024,640]{1,0:T(8,128)(2,1)} %copy.32, bf16[]{:T(256)} %constant.150.clone.1), kind=kCustom, calls=%fused_computation.24 | custom fusion | bytes 5243392 | tf_op jit(solution)/shard_map/scatter | solution.py:149
  (95 shorter events, 97.1 us)
Async XLA Ops:
  6.5 555.4 %copy-start = (bf16[640,2560]{1,0:T(8,128)(2,1)S(1)}, bf16[640,2560]{1,0:T(8,128)(2,1)}, u32[]{:S(2)}) copy-start(bf16[640,2560]{1,0:T(8,128)(2,1)} %param.7) | copy-start | bytes 9830404
  89.8 31.1 %all-to-all-start = ((bf16[32,32,640]{2,1,0:T(8,128)(2,1)}), bf16[32,32,640]{2,1,0:T(8,128)(2,1)}, u32[]{:S(2)}, u32[]{:S(2)}) async-start(bf16[32,32,640]{2,1,0:T(8,128)(2,1)} %bitcast.60), calls=%async_computation | async-start | bytes 2621440 | tf_op jit(solution)/shard_map/all_to_all | solution.py:47
  102.0 58.2 %all-gather.3.cloned.1.call-start = ((), (), s32[]{:S(2)}) async-start(), calls=%async_computation.3 | async-start | bytes 3276800 | tf_op jit(solution)/shard_map/all_gather | solution.py:23
  171.8 2.1 copy-start.4
  203.1 55.2 %all-to-all-start.1 = ((bf16[32,32,1920]{2,1,0:T(8,128)(2,1)}), bf16[32,32,1920]{2,1,0:T(8,128)(2,1)}, u32[]{:S(2)}, u32[]{:S(2)}) async-start(bf16[32,32,1920]{2,1,0:T(8,128)(2,1)} %bitcast.51), calls=%async_computation.1 | async-start | bytes 7864320 | tf_op jit(solution)/shard_map/all_to_all | solution.py:47
  210.9 420.0 %reduce-scatter.4.cloned.1.call-start = ((), (), s32[]{:S(2)}) async-start(), calls=%async_computation.4 | async-start | bytes 6553600
  271.2 60.1 %collective-permute-start = (bf16[1024,1280]{1,0:T(8,128)(2,1)S(1)}, bf16[1024,1280]{1,0:T(8,128)(2,1)S(1)}, u32[]{:S(2)}, u32[]{:S(2)}) collective-permute-start(bf16[1024,1280]{1,0:T(8,128)(2,1)S(1)} %slice.66), channel_id=1, source_target_pairs={{0,4},{4,8},{8,12},{12,0},{1,5},{5,9},{9,13},{13,1},{2,6},{6,10},{... | collective-permute-start | bytes 7864328 | tf_op jit(solution)/shard_map/ppermute | solution.py:109
  331.3 1.5 copy-start.2
  332.8 58.2 %collective-permute-start.1 = (bf16[1024,1280]{1,0:T(8,128)(2,1)S(1)}, bf16[1024,1280]{1,0:T(8,128)(2,1)}, u32[]{:S(2)}, u32[]{:S(2)}) collective-permute-start(bf16[1024,1280]{1,0:T(8,128)(2,1)S(1)} %collective-permute-done), channel_id=1, source_target_pairs={{0,4},{4,8},{8,12},{12,0},{1,5},{5,9},{9,13},{13,1},{2,6},{6,10},{... | collective-permute-start | bytes 7864328 | tf_op jit(solution)/shard_map/ppermute | solution.py:109
  391.0 57.5 %collective-permute-start.2 = (bf16[1024,1280]{1,0:T(8,128)(2,1)}, bf16[1024,1280]{1,0:T(8,128)(2,1)}, u32[]{:S(2)}, u32[]{:S(2)}) collective-permute-start(bf16[1024,1280]{1,0:T(8,128)(2,1)} %collective-permute-done.1), channel_id=1, source_target_pairs={{0,4},{4,8},{8,12},{12,0},{1,5},{5,9},{9,13},{13,1},{2,6},{6,10},{... | collective-permute-start | bytes 7864328 | tf_op jit(solution)/shard_map/ppermute | solution.py:109
  452.0 3.6 copy-start.3
  455.6 3.1 copy-start.1
Sparse Core Ops, SparseCore 0:
  125.4 34.7 all-gather.2
  576.1 54.7 reduce-scatter.3
